TPU v7x, 32 devices: a whole 2x2x4 slice. The times are simulated.
32 devices in a mesh: dp: 16 (over z, y, x), inner: 2 (over core).
Axes of the slice: x: 2, y: 2, z: 4, core: 2. Of those that a mesh axis runs over, the one named last changes fastest.
Arguments:
- features: bfloat16 [8192, 2048], P(('dp', 'inner')), may hold values from -12 to 12
- kv_cotangent: bfloat16 [8192, 512], P(('dp', 'inner')), may hold values from -0.0625 to 0.0625
- owner_of_block: int32 [64], replicated, may hold values from 0 to 15, as said below
- first_moment: float32 [16, 4, 128, 128], P('dp'), may hold values from -1.25 to 1.25
- second_moment: float32 [16, 4, 128, 128], P('dp'), may hold values from 0.05 to 1
- left_stat: float32 [16, 4, 128, 128], P('dp')
- right_stat: float32 [16, 4, 128, 128], P('dp')
- left_basis: bfloat16 [16, 4, 128, 128], P('dp')
- right_basis: bfloat16 [16, 4, 128, 128], P('dp')
Outputs:
- update: bfloat16 [2048, 512], replicated
- new_left_basis: bfloat16 [16, 4, 128, 128], P('dp')
- new_right_basis: bfloat16 [16, 4, 128, 128], P('dp')
Inputs may be any that keep to these rules, and one draw needn't show every extreme that they name: `owner_of_block`: each index of dp owns at most 4 tiles, and one index owns exactly 4.
All inputs are finite; a program needn't handle non-finite values.
Results may differ from a plain program's by a relative error of at most 0.001.
Values may be sent and summed in bfloat16 or wider, within the bound.
No kernel may reach another device: no remote copies, remote signals or barrier semaphores. Data moves between devices by JAX's collectives and lax.ppermute only.
A program may use at most 64 MiB of HBM per device.

v0:
```python
import jax
import jax.numpy as jnp
from jax import lax
from jax.sharding import PartitionSpec as P

NS_STEPS = 12
highest = lax.Precision.HIGHEST


def rotate_in(basis_left, matrix, basis_right):
    half = jnp.einsum("sji,sjk->sik", basis_left, matrix, precision=highest)
    return jnp.einsum("sij,sjk->sik", half, basis_right, precision=highest)


def rotate_out(basis_left, matrix, basis_right):
    half = jnp.einsum("sij,sjk->sik", basis_left, matrix, precision=highest)
    return jnp.einsum("sij,skj->sik", half, basis_right, precision=highest)


def orthogonalize(stat, basis):
    power = jnp.einsum("sij,sjk->sik", stat, basis, precision=highest)
    scale = jnp.sqrt(jnp.sum(power * power, axis=(1, 2), keepdims=True) + 1e-06)
    iterate = power / scale
    for sweep in range(NS_STEPS):
        gram = jnp.einsum("sji,sjk->sik", iterate, iterate, precision=highest)
        iterate = 1.5 * iterate - 0.5 * jnp.einsum("sij,sjk->sik", iterate, gram, precision=highest)
    return iterate


def soap_tiles(grads, first, second, stat_left, stat_right, basis_left, basis_right):
    rotated = rotate_in(basis_left, grads, basis_right)
    moment = 0.95 * first + 0.05 * grads
    moment_rot = rotate_in(basis_left, moment, basis_right)
    second_new = 0.95 * second + 0.05 * rotated * rotated
    direction = rotate_out(basis_left, moment_rot / (jnp.sqrt(second_new) + 1e-08), basis_right)
    left_new = 0.95 * stat_left + 0.05 * jnp.einsum("sij,skj->sik", grads, grads, precision=highest)
    right_new = 0.95 * stat_right + 0.05 * jnp.einsum(
        "sji,sjk->sik", grads, grads, precision=highest
    )
    return (direction, orthogonalize(left_new, basis_left), orthogonalize(right_new, basis_right))


def per_device(
    features,
    kv_cotangent,
    owner_of_block,
    first_moment,
    second_moment,
    left_stat,
    right_stat,
    left_basis,
    right_basis,
):
    tile = left_basis.shape[-1]
    capacity = left_basis.shape[1]
    d_win = features.shape[1]
    width = kv_cotangent.shape[1]
    row_tiles = d_win // tile
    col_tiles = width // tile
    nblocks = owner_of_block.shape[0]
    owner_here = lax.axis_index("dp")
    block_ids = jnp.arange(nblocks, dtype=jnp.int32)
    same = owner_of_block[:, None] == owner_of_block[None, :]
    earlier = block_ids[None, :] < block_ids[:, None]
    slot = jnp.sum((same & earlier).astype(jnp.int32), axis=1)
    slot_ids = jnp.arange(capacity, dtype=jnp.int32)
    match = (owner_of_block[None, :] == owner_here) & (slot[None, :] == slot_ids[:, None])
    live = jnp.any(match, axis=1)
    which = jnp.sum(jnp.where(match, block_ids[None, :], 0), axis=1)
    row_start = which // col_tiles * tile
    col_start = which % col_tiles * tile
    partial_grad = lax.dot_general(
        features, kv_cotangent, (((0,), (0,)), ((), ())), preferred_element_type=jnp.float32
    )
    grad = lax.psum(partial_grad, ("dp", "inner"))
    fetched = [
        lax.dynamic_slice(grad, (row_start[slot_index], col_start[slot_index]), (tile, tile))
        for slot_index in range(capacity)
    ]
    grads = jnp.stack(fetched)
    basis_left = left_basis[0].astype(jnp.float32)
    basis_right = right_basis[0].astype(jnp.float32)
    direction, left_iter, right_iter = soap_tiles(
        grads,
        first_moment[0],
        second_moment[0],
        left_stat[0],
        right_stat[0],
        basis_left,
        basis_right,
    )
    direction_low = direction.astype(jnp.bfloat16)
    everyone = lax.all_gather(direction_low[None], "dp", axis=0, tiled=True)
    tiles = everyone[owner_of_block, slot]
    update = (
        tiles.reshape(row_tiles, col_tiles, tile, tile).transpose(0, 2, 1, 3).reshape(d_win, width)
    )
    keep = live[:, None, None]
    new_left = jnp.where(keep, left_iter.astype(jnp.bfloat16), left_basis[0])
    new_right = jnp.where(keep, right_iter.astype(jnp.bfloat16), right_basis[0])
    return (update, new_left[None], new_right[None])


def solution(mesh):
    return jax.shard_map(
        per_device,
        mesh=mesh,
        in_specs=(
            P(("dp", "inner"), None),
            P(("dp", "inner"), None),
            P(),
            P("dp", None, None, None),
            P("dp", None, None, None),
            P("dp", None, None, None),
            P("dp", None, None, None),
            P("dp", None, None, None),
            P("dp", None, None, None),
        ),
        out_specs=(P(), P("dp", None, None, None), P("dp", None, None, None)),
        check_vma=False,
    )
```

profile of v0, /device:TPU:0, one launch (start us, length us, event | category | flops | bytes accessed | tf_op | source)
XLA Modules:
  0.0 234.5 jit_solution(13853577143957279118)
XLA Ops:
  7.2 1.2 copy-done
  8.4 3.6 %fusion.71 = f32[2048,512]{1,0:T(8,128)} fusion(bf16[256,2048]{1,0:T(8,128)(2,1)S(1)} %copy-done, bf16[256,512]{1,0:T(8,128)(2,1)} %param.10), kind=kOutput, calls=%fused_computation.126 | convolution fusion | flops 536870912 | bytes 5505024 | tf_op jit(solution)/shard_map/dot_general | solution.py:72
  13.0 0.7 fusion.69
  28.8 129.2 %all-reduce.2.cloned.1.call-done = f32[2048,512]{1,0:T(8,128)} async-done(((f32[2048,512]{1,0:T(8,128)}), f32[2048,512]{1,0:T(8,128)}) %all-reduce.2.cloned.1.call-update) | async-done | bytes 4194320 | tf_op jit(solution)/shard_map/psum | solution.py:75
  158.0 1.1 dynamic-slice_bitcast_fusion.3
  160.7 1.0 convolution_convert_fusion
  161.8 0.7 fusion.25
  162.8 0.7 fusion.53
  164.0 0.6 fusion.72
  166.0 0.6 fusion.74
  168.1 0.6 fusion.76
  169.1 0.6 fusion.77
  172.1 0.6 fusion.80
  175.0 0.6 fusion.12
  175.9 0.7 fusion.54
  180.1 1.1 fusion.31
  182.2 0.6 fusion.87
  184.3 0.6 fusion.89
  187.3 0.8 fusion.92
  189.2 1.1 fusion.29
  190.3 31.4 %all-gather.3.cloned.1.call-done = bf16[64,128,128]{2,1,0:T(8,128)(2,1)} async-done(((bf16[4,128,128]{2,1,0:T(8,128)(2,1)}), bf16[64,128,128]{2,1,0:T(8,128)(2,1)}) %all-gather.3.cloned.1.call-update) | async-done | bytes 2097168 | tf_op jit(solution)/shard_map/all_gather | solution.py:93
  221.7 2.5 %gather_fusion = bf16[64,128,128]{2,1,0:T(8,128)(2,1)S(1)} fusion(bf16[16,4,128,128]{3,2,1,0:T(8,128)(2,1)} %bitcast.173, s32[64]{0:T(128)S(1)} %fusion.65), kind=kCustom, calls=%fused_computation | custom fusion | bytes 4194816 | tf_op jit(solution)/shard_map/gather | solution.py:94
  224.2 1.8 copy.20
  226.0 1.7 copy.79
  (70 shorter events, 20.9 us)
Async XLA Ops:
  7.2 1.2 copy-start
  7.2 150.8 %all-reduce.2.cloned.1.call-start = ((), (), s32[]{:S(2)}) async-start(), calls=%async_computation | async-start | bytes 8388608 | tf_op jit(solution)/shard_map/psum | solution.py:75
  12.0 0.7 copy-start.7
  12.0 147.1 %copy-start.1 = (bf16[1,4,128,128]{3,2,1,0:T(8,128)(2,1)S(1)}, bf16[1,4,128,128]{3,2,1,0:T(8,128)(2,1)}, u32[]{:S(2)}) copy-start(bf16[1,4,128,128]{3,2,1,0:T(8,128)(2,1)} %param.16) | copy-start | bytes 393220
  12.0 147.5 %copy-start.3 = (f32[1,4,128,128]{3,2,1,0:T(8,128)S(1)}, f32[1,4,128,128]{3,2,1,0:T(8,128)}, u32[]{:S(2)}) copy-start(f32[1,4,128,128]{3,2,1,0:T(8,128)} %param.12) | copy-start | bytes 786436
  12.1 147.8 %copy-start.2 = (bf16[1,4,128,128]{3,2,1,0:T(8,128)(2,1)S(1)}, bf16[1,4,128,128]{3,2,1,0:T(8,128)(2,1)}, u32[]{:S(2)}) copy-start(bf16[1,4,128,128]{3,2,1,0:T(8,128)(2,1)} %param.17) | copy-start | bytes 393220
  12.1 148.0 %copy-start.6 = (f32[1,4,128,128]{3,2,1,0:T(8,128)S(1)}, f32[1,4,128,128]{3,2,1,0:T(8,128)}, u32[]{:S(2)}) copy-start(f32[1,4,128,128]{3,2,1,0:T(8,128)} %param.13) | copy-start | bytes 786436
  12.1 209.6 %all-gather.3.cloned.1.call-start = ((), (), s32[]{:S(2)}) async-start(), calls=%async_computation.1 | async-start | bytes 2228224 | tf_op jit(solution)/shard_map/all_gather | solution.py:93
  159.5 2.3 copy-start.4
  172.1 2.8 %copy-start.5 = (f32[1,4,128,128]{3,2,1,0:T(8,128)S(1)}, f32[1,4,128,128]{3,2,1,0:T(8,128)}, u32[]{:S(2)}) copy-start(f32[1,4,128,128]{3,2,1,0:T(8,128)} %param.15) | copy-start | bytes 786436
Sparse Core Ops, SparseCore 0:
  13.5 144.4 all-reduce.1
  161.9 59.6 all-gather.2
where the time goes:
time: 235 us
  waiting for transfers between devices  161 us (69%)
  matrix products  34.2 us (15%)
  between operations  29.5 us (13%)
  local copies, waits for them, and re-layouts  9.58 us (4%)
    psum x1, waiting for transfers between devices, per_device(): grad = lax.psum(partial_grad, ('dp', 'inner'))  129 us
    all_gather x1, waiting for transfers between devices, per_device(): everyone = lax.all_gather(direction_low[None], 'dp', axis=0, tiled=True)  31.4 us
    dot_general x24, matrix products, orthogonalize(): gram = jnp.einsum('sji,sjk->sik', iterate, iterate, precision=highest)  14.8 us
    dot_general x24, matrix products, orthogonalize(): jnp.einsum('sij,sjk->sik', iterate, gram, precision=highest)  11.3 us
  transfers between devices with their start and end apart: 2, of which 2 were waited for; matrix products, arithmetic and copies ran while one was open for 12% of the time, Pallas kernels for 0%

commit v1 on v0

--- a/solution.py
+++ b/solution.py
@@ -51,6 +51,36 @@
     left_basis,
     right_basis,
 ):
+
+    def write_group_over_axis(m):
+        f_now = lax.axis_size("dp")
+        local_now = lax.axis_index("dp")
+        latest, shaped, oldest = (f_now, local_now, m.shape[0])
+        items = []
+        for kk, p in enumerate(m.shape):
+            items.append(p * latest if kk == 0 else p)
+        upper = lax.dynamic_update_slice_in_dim(
+            jnp.zeros(items, m.dtype), m, shaped * oldest, axis=0
+        )
+        z_new = y1 = m
+        for jj in [*range(1, latest // 2 + 1)]:
+            gallery = []
+            for kk in [*range(latest)]:
+                gallery.append((kk, (kk + 1) % latest))
+            z_new = lax.ppermute(z_new, "dp", gallery)
+            upper = lax.dynamic_update_slice_in_dim(
+                upper, z_new, (shaped - jj) % latest * oldest, axis=0
+            )
+            if 2 * jj < latest:
+                all_rows = []
+                for kk in [*range(latest)]:
+                    all_rows.append((kk, (kk - 1) % latest))
+                y1 = lax.ppermute(y1, axis_name="dp", perm=all_rows)
+                upper = lax.dynamic_update_slice_in_dim(
+                    upper, y1, (shaped + jj) % latest * oldest, axis=0
+                )
+        return upper
+
     tile = left_basis.shape[-1]
     capacity = left_basis.shape[1]
     d_win = features.shape[1]
@@ -90,7 +120,7 @@
         basis_right,
     )
     direction_low = direction.astype(jnp.bfloat16)
-    everyone = lax.all_gather(direction_low[None], "dp", axis=0, tiled=True)
+    everyone = write_group_over_axis(direction_low[None])
     tiles = everyone[owner_of_block, slot]
     update = (
         tiles.reshape(row_tiles, col_tiles, tile, tile).transpose(0, 2, 1, 3).reshape(d_win, width)

time: 235 us -> 272 us (1.16)
  starting transfers between devices: 0.08 us -> 39.9 us
  waiting for transfers between devices: 161 us -> 157 us
    ppermute x0 -> x15, starting transfers between devices: none -> 39.8 us  [the longest x7 38.2 us: write_group_over_axis(): y1 = lax.ppermute(y1, axis_name='dp', perm=all_rows)]
    all_gather x1 -> x0, waiting for transfers between devices: 31.4 us -> none  [per_device(): everyone = lax.all_gather(direction_low[None], 'dp', axis=0, tiled=True)]
    ppermute x0 -> x15, waiting for transfers between devices: none -> 27.5 us  [the longest x8 27.5 us: write_group_over_axis(): z_new = lax.ppermute(z_new, 'dp', gallery)]
    unnamed x17 -> x18, local copies, waits for them, and re-layouts: 3.44 us -> 6.85 us
  transfers between devices with their start and end apart: 2 -> 16, of which waited for: 2 -> 8; matrix products, arithmetic and copies ran while one was open for 12% -> 11% of each run, Pallas kernels for 0% -> 0%
where the time goes in v1:
time: 272 us
  waiting for transfers between devices  157 us (58%)
  starting transfers between devices  39.9 us (15%)
  matrix products  33.3 us (12%)
  between operations  29.6 us (11%)
  local copies, waits for them, and re-layouts  11.6 us (4%)
    psum x1, waiting for transfers between devices, per_device(): grad = lax.psum(partial_grad, ('dp', 'inner'))  129 us
    ppermute x7, starting transfers between devices, write_group_over_axis(): y1 = lax.ppermute(y1, axis_name='dp', perm=all_rows)  38.2 us
    ppermute x8, waiting for transfers between devices, write_group_over_axis(): z_new = lax.ppermute(z_new, 'dp', gallery)  27.5 us
    dot_general x24, matrix products, orthogonalize(): gram = jnp.einsum('sji,sjk->sik', iterate, iterate, precision=highest)  14.5 us
    dot_general x24, matrix products, orthogonalize(): jnp.einsum('sij,sjk->sik', iterate, gram, precision=highest)  11.1 us
    unnamed x18, local copies, waits for them, and re-layouts  6.85 us
  transfers between devices with their start and end apart: 16, of which 8 were waited for; matrix products, arithmetic and copies ran while one was open for 11% of the time, Pallas kernels for 0%

profile of v1, /device:TPU:0, one launch (start us, length us, event | category | flops | bytes accessed | tf_op | source)
XLA Modules:
  0.0 271.7 jit_solution(17220127413089115059)
XLA Ops:
  7.2 1.2 copy-done
  8.4 3.7 %fusion.72 = f32[2048,512]{1,0:T(8,128)} fusion(bf16[256,2048]{1,0:T(8,128)(2,1)S(1)} %copy-done, bf16[256,512]{1,0:T(8,128)(2,1)} %param.10), kind=kOutput, calls=%fused_computation.143 | convolution fusion | flops 536870912 | bytes 5505024 | tf_op jit(solution)/shard_map/dot_general | solution.py:102
  28.7 129.3 %all-reduce.2.cloned.1.call-done = f32[2048,512]{1,0:T(8,128)} async-done(((f32[2048,512]{1,0:T(8,128)}), f32[2048,512]{1,0:T(8,128)}) %all-reduce.2.cloned.1.call-update) | async-done | bytes 4194320 | tf_op jit(solution)/shard_map/psum | solution.py:105
  158.0 1.1 dynamic-slice_bitcast_fusion.3
  161.6 1.6 collective-permute-start
  163.2 4.1 %collective-permute-start.1 = (bf16[1,4,128,128]{3,2,1,0:T(8,128)(2,1)S(1)}, bf16[1,4,128,128]{3,2,1,0:T(8,128)(2,1)S(1)}, u32[]{:S(2)}, u32[]{:S(2)}) collective-permute-start(bf16[1,4,128,128]{3,2,1,0:T(8,128)(2,1)S(1)} %get-tuple-element.24), channel_id=1, source_target_pairs={{0,30},{2,0},{4,2},{6,4},{8,6},{10,8},{12,10},{14,12},{16,14},{18,... | collective-permute-start | bytes 393224 | tf_op jit(solution)/shard_map/ppermute | solution.py:78
  193.4 1.1 fusion.30
  194.5 1.1 fusion.32
  195.6 5.6 %collective-permute-start.3 = (bf16[1,4,128,128]{3,2,1,0:T(8,128)(2,1)S(1)}, bf16[1,4,128,128]{3,2,1,0:T(8,128)(2,1)S(1)}, u32[]{:S(2)}, u32[]{:S(2)}) collective-permute-start(bf16[1,4,128,128]{3,2,1,0:T(8,128)(2,1)S(1)} %collective-permute-done.1), channel_id=1, source_target_pairs={{0,30},{2,0},{4,2},{6,4},{8,6},{10,8},{12,10},{14,12},{16,14},{18,... | collective-permute-start | bytes 393224 | tf_op jit(solution)/shard_map/ppermute | solution.py:78
  201.2 2.9 %collective-permute-done.2 = bf16[1,4,128,128]{3,2,1,0:T(8,128)(2,1)S(1)} collective-permute-done((bf16[1,4,128,128]{3,2,1,0:T(8,128)(2,1)S(1)}, bf16[1,4,128,128]{3,2,1,0:T(8,128)(2,1)S(1)}, u32[]{:S(2)}, u32[]{:S(2)}) %collective-permute-start.2) | collective-permute-done | bytes 131104 | tf_op jit(solution)/shard_map/ppermute | solution.py:70
  204.1 5.7 %collective-permute-start.5 = (bf16[1,4,128,128]{3,2,1,0:T(8,128)(2,1)S(1)}, bf16[1,4,128,128]{3,2,1,0:T(8,128)(2,1)S(1)}, u32[]{:S(2)}, u32[]{:S(2)}) collective-permute-start(bf16[1,4,128,128]{3,2,1,0:T(8,128)(2,1)S(1)} %collective-permute-done.3), channel_id=1, source_target_pairs={{0,30},{2,0},{4,2},{6,4},{8,6},{10,8},{12,10},{14,12},{16,14},{18,... | collective-permute-start | bytes 393224 | tf_op jit(solution)/shard_map/ppermute | solution.py:78
  209.9 2.8 %collective-permute-done.4 = bf16[1,4,128,128]{3,2,1,0:T(8,128)(2,1)S(1)} collective-permute-done((bf16[1,4,128,128]{3,2,1,0:T(8,128)(2,1)S(1)}, bf16[1,4,128,128]{3,2,1,0:T(8,128)(2,1)S(1)}, u32[]{:S(2)}, u32[]{:S(2)}) %collective-permute-start.4) | collective-permute-done | bytes 131104 | tf_op jit(solution)/shard_map/ppermute | solution.py:70
  212.7 5.7 %collective-permute-start.7 = (bf16[1,4,128,128]{3,2,1,0:T(8,128)(2,1)S(1)}, bf16[1,4,128,128]{3,2,1,0:T(8,128)(2,1)S(1)}, u32[]{:S(2)}, u32[]{:S(2)}) collective-permute-start(bf16[1,4,128,128]{3,2,1,0:T(8,128)(2,1)S(1)} %collective-permute-done.5), channel_id=1, source_target_pairs={{0,30},{2,0},{4,2},{6,4},{8,6},{10,8},{12,10},{14,12},{16,14},{18,... | collective-permute-start | bytes 393224 | tf_op jit(solution)/shard_map/ppermute | solution.py:78
  218.5 2.9 %collective-permute-done.6 = bf16[1,4,128,128]{3,2,1,0:T(8,128)(2,1)S(1)} collective-permute-done((bf16[1,4,128,128]{3,2,1,0:T(8,128)(2,1)S(1)}, bf16[1,4,128,128]{3,2,1,0:T(8,128)(2,1)S(1)}, u32[]{:S(2)}, u32[]{:S(2)}) %collective-permute-start.6) | collective-permute-done | bytes 131104 | tf_op jit(solution)/shard_map/ppermute | solution.py:70
  221.4 5.6 %collective-permute-start.9 = (bf16[1,4,128,128]{3,2,1,0:T(8,128)(2,1)S(1)}, bf16[1,4,128,128]{3,2,1,0:T(8,128)(2,1)S(1)}, u32[]{:S(2)}, u32[]{:S(2)}) collective-permute-start(bf16[1,4,128,128]{3,2,1,0:T(8,128)(2,1)S(1)} %collective-permute-done.7), channel_id=1, source_target_pairs={{0,30},{2,0},{4,2},{6,4},{8,6},{10,8},{12,10},{14,12},{16,14},{18,... | collective-permute-start | bytes 393224 | tf_op jit(solution)/shard_map/ppermute | solution.py:78
  227.1 3.7 %collective-permute-done.8 = bf16[1,4,128,128]{3,2,1,0:T(8,128)(2,1)S(1)} collective-permute-done((bf16[1,4,128,128]{3,2,1,0:T(8,128)(2,1)S(1)}, bf16[1,4,128,128]{3,2,1,0:T(8,128)(2,1)S(1)}, u32[]{:S(2)}, u32[]{:S(2)}) %collective-permute-start.8) | collective-permute-done | bytes 131104 | tf_op jit(solution)/shard_map/ppermute | solution.py:70
  230.8 5.9 %collective-permute-start.11 = (bf16[1,4,128,128]{3,2,1,0:T(8,128)(2,1)S(1)}, bf16[1,4,128,128]{3,2,1,0:T(8,128)(2,1)S(1)}, u32[]{:S(2)}, u32[]{:S(2)}) collective-permute-start(bf16[1,4,128,128]{3,2,1,0:T(8,128)(2,1)S(1)} %collective-permute-done.9), channel_id=1, source_target_pairs={{0,30},{2,0},{4,2},{6,4},{8,6},{10,8},{12,10},{14,12},{16,14},{18,... | collective-permute-start | bytes 393224 | tf_op jit(solution)/shard_map/ppermute | solution.py:78
  236.7 3.7 %collective-permute-done.10 = bf16[1,4,128,128]{3,2,1,0:T(8,128)(2,1)S(1)} collective-permute-done((bf16[1,4,128,128]{3,2,1,0:T(8,128)(2,1)S(1)}, bf16[1,4,128,128]{3,2,1,0:T(8,128)(2,1)S(1)}, u32[]{:S(2)}, u32[]{:S(2)}) %collective-permute-start.10) | collective-permute-done | bytes 131104 | tf_op jit(solution)/shard_map/ppermute | solution.py:70
  240.4 5.6 %collective-permute-start.13 = (bf16[1,4,128,128]{3,2,1,0:T(8,128)(2,1)S(1)}, bf16[1,4,128,128]{3,2,1,0:T(8,128)(2,1)S(1)}, u32[]{:S(2)}, u32[]{:S(2)}) collective-permute-start(bf16[1,4,128,128]{3,2,1,0:T(8,128)(2,1)S(1)} %collective-permute-done.11), channel_id=1, source_target_pairs={{0,30},{2,0},{4,2},{6,4},{8,6},{10,8},{12,10},{14,12},{16,14},{18,... | collective-permute-start | bytes 393224 | tf_op jit(solution)/shard_map/ppermute | solution.py:78
  246.1 3.0 %collective-permute-done.12 = bf16[1,4,128,128]{3,2,1,0:T(8,128)(2,1)S(1)} collective-permute-done((bf16[1,4,128,128]{3,2,1,0:T(8,128)(2,1)S(1)}, bf16[1,4,128,128]{3,2,1,0:T(8,128)(2,1)S(1)}, u32[]{:S(2)}, u32[]{:S(2)}) %collective-permute-start.12) | collective-permute-done | bytes 131104 | tf_op jit(solution)/shard_map/ppermute | solution.py:70
  249.1 8.5 %collective-permute-done.14 = bf16[1,4,128,128]{3,2,1,0:T(8,128)(2,1)S(1)} collective-permute-done((bf16[1,4,128,128]{3,2,1,0:T(8,128)(2,1)S(1)}, bf16[1,4,128,128]{3,2,1,0:T(8,128)(2,1)S(1)}, u32[]{:S(2)}, u32[]{:S(2)}) %collective-permute-start.14) | collective-permute-done | bytes 131104 | tf_op jit(solution)/shard_map/ppermute | solution.py:70
  257.6 2.1 gather_fusion
  259.8 3.4 %copy.109 = bf16[16,128,4,128]{3,2,1,0:T(4,128)(2,1)S(1)} copy(bf16[16,128,4,128]{3,1,2,0:T(8,128)(2,1)} %bitcast.175) | data formatting | bytes 4194304
  263.2 1.7 copy.113
  (113 shorter events, 30.1 us)
Async XLA Ops:
  7.2 1.2 copy-start
  7.2 150.8 %all-reduce.2.cloned.1.call-start = ((), (), s32[]{:S(2)}) async-start(), calls=%async_computation | async-start | bytes 8388608 | tf_op jit(solution)/shard_map/psum | solution.py:105
  12.1 0.7 copy-start.7
  12.1 147.1 %copy-start.1 = (bf16[1,4,128,128]{3,2,1,0:T(8,128)(2,1)S(1)}, bf16[1,4,128,128]{3,2,1,0:T(8,128)(2,1)}, u32[]{:S(2)}) copy-start(bf16[1,4,128,128]{3,2,1,0:T(8,128)(2,1)} %param.16) | copy-start | bytes 393220
  12.1 147.5 %copy-start.3 = (f32[1,4,128,128]{3,2,1,0:T(8,128)S(1)}, f32[1,4,128,128]{3,2,1,0:T(8,128)}, u32[]{:S(2)}) copy-start(f32[1,4,128,128]{3,2,1,0:T(8,128)} %param.12) | copy-start | bytes 786436
  12.1 147.8 %copy-start.2 = (bf16[1,4,128,128]{3,2,1,0:T(8,128)(2,1)S(1)}, bf16[1,4,128,128]{3,2,1,0:T(8,128)(2,1)}, u32[]{:S(2)}) copy-start(bf16[1,4,128,128]{3,2,1,0:T(8,128)(2,1)} %param.17) | copy-start | bytes 393220
  12.1 148.0 %copy-start.6 = (f32[1,4,128,128]{3,2,1,0:T(8,128)S(1)}, f32[1,4,128,128]{3,2,1,0:T(8,128)}, u32[]{:S(2)}) copy-start(f32[1,4,128,128]{3,2,1,0:T(8,128)} %param.13) | copy-start | bytes 786436
  160.1 7.2 %copy-start.4 = (f32[1,4,128,128]{3,2,1,0:T(8,128)S(1)}, f32[1,4,128,128]{3,2,1,0:T(8,128)}, u32[]{:S(2)}) copy-start(f32[1,4,128,128]{3,2,1,0:T(8,128)} %param.15) | copy-start | bytes 786436
  161.6 33.9 %collective-permute-start = (bf16[1,4,128,128]{3,2,1,0:T(8,128)(2,1)S(1)}, bf16[1,4,128,128]{3,2,1,0:T(8,128)(2,1)S(1)}, u32[]{:S(2)}, u32[]{:S(2)}) collective-permute-start(bf16[1,4,128,128]{3,2,1,0:T(8,128)(2,1)S(1)} %get-tuple-element.24), channel_id=1, source_target_pairs={{0,2},{2,4},{4,6},{6,8},{8,10},{10,12},{12,14},{14,16},{16,18},{18... | collective-permute-start | bytes 393224 | tf_op jit(solution)/shard_map/ppermute | solution.py:70
  163.2 32.3 %collective-permute-start.1 = (bf16[1,4,128,128]{3,2,1,0:T(8,128)(2,1)S(1)}, bf16[1,4,128,128]{3,2,1,0:T(8,128)(2,1)S(1)}, u32[]{:S(2)}, u32[]{:S(2)}) collective-permute-start(bf16[1,4,128,128]{3,2,1,0:T(8,128)(2,1)S(1)} %get-tuple-element.24), channel_id=1, source_target_pairs={{0,30},{2,0},{4,2},{6,4},{8,6},{10,8},{12,10},{14,12},{16,14},{18,... | collective-permute-start | bytes 393224 | tf_op jit(solution)/shard_map/ppermute | solution.py:78
  177.6 2.7 copy-start.5
  195.6 8.6 %collective-permute-start.2 = (bf16[1,4,128,128]{3,2,1,0:T(8,128)(2,1)S(1)}, bf16[1,4,128,128]{3,2,1,0:T(8,128)(2,1)S(1)}, u32[]{:S(2)}, u32[]{:S(2)}) collective-permute-start(bf16[1,4,128,128]{3,2,1,0:T(8,128)(2,1)S(1)} %collective-permute-done), channel_id=1, source_target_pairs={{0,2},{2,4},{4,6},{6,8},{8,10},{10,12},{12,14},{14,16},{16,18},{18... | collective-permute-start | bytes 393224 | tf_op jit(solution)/shard_map/ppermute | solution.py:70
  195.6 8.6 %collective-permute-start.3 = (bf16[1,4,128,128]{3,2,1,0:T(8,128)(2,1)S(1)}, bf16[1,4,128,128]{3,2,1,0:T(8,128)(2,1)S(1)}, u32[]{:S(2)}, u32[]{:S(2)}) collective-permute-start(bf16[1,4,128,128]{3,2,1,0:T(8,128)(2,1)S(1)} %collective-permute-done.1), channel_id=1, source_target_pairs={{0,30},{2,0},{4,2},{6,4},{8,6},{10,8},{12,10},{14,12},{16,14},{18,... | collective-permute-start | bytes 393224 | tf_op jit(solution)/shard_map/ppermute | solution.py:78
  204.1 8.6 %collective-permute-start.4 = (bf16[1,4,128,128]{3,2,1,0:T(8,128)(2,1)S(1)}, bf16[1,4,128,128]{3,2,1,0:T(8,128)(2,1)S(1)}, u32[]{:S(2)}, u32[]{:S(2)}) collective-permute-start(bf16[1,4,128,128]{3,2,1,0:T(8,128)(2,1)S(1)} %collective-permute-done.2), channel_id=1, source_target_pairs={{0,2},{2,4},{4,6},{6,8},{8,10},{10,12},{12,14},{14,16},{16,18},{18... | collective-permute-start | bytes 393224 | tf_op jit(solution)/shard_map/ppermute | solution.py:70
  204.1 8.6 %collective-permute-start.5 = (bf16[1,4,128,128]{3,2,1,0:T(8,128)(2,1)S(1)}, bf16[1,4,128,128]{3,2,1,0:T(8,128)(2,1)S(1)}, u32[]{:S(2)}, u32[]{:S(2)}) collective-permute-start(bf16[1,4,128,128]{3,2,1,0:T(8,128)(2,1)S(1)} %collective-permute-done.3), channel_id=1, source_target_pairs={{0,30},{2,0},{4,2},{6,4},{8,6},{10,8},{12,10},{14,12},{16,14},{18,... | collective-permute-start | bytes 393224 | tf_op jit(solution)/shard_map/ppermute | solution.py:78
  212.7 8.7 %collective-permute-start.6 = (bf16[1,4,128,128]{3,2,1,0:T(8,128)(2,1)S(1)}, bf16[1,4,128,128]{3,2,1,0:T(8,128)(2,1)S(1)}, u32[]{:S(2)}, u32[]{:S(2)}) collective-permute-start(bf16[1,4,128,128]{3,2,1,0:T(8,128)(2,1)S(1)} %collective-permute-done.4), channel_id=1, source_target_pairs={{0,2},{2,4},{4,6},{6,8},{8,10},{10,12},{12,14},{14,16},{16,18},{18... | collective-permute-start | bytes 393224 | tf_op jit(solution)/shard_map/ppermute | solution.py:70
  212.7 8.7 %collective-permute-start.7 = (bf16[1,4,128,128]{3,2,1,0:T(8,128)(2,1)S(1)}, bf16[1,4,128,128]{3,2,1,0:T(8,128)(2,1)S(1)}, u32[]{:S(2)}, u32[]{:S(2)}) collective-permute-start(bf16[1,4,128,128]{3,2,1,0:T(8,128)(2,1)S(1)} %collective-permute-done.5), channel_id=1, source_target_pairs={{0,30},{2,0},{4,2},{6,4},{8,6},{10,8},{12,10},{14,12},{16,14},{18,... | collective-permute-start | bytes 393224 | tf_op jit(solution)/shard_map/ppermute | solution.py:78
  221.4 9.4 %collective-permute-start.8 = (bf16[1,4,128,128]{3,2,1,0:T(8,128)(2,1)S(1)}, bf16[1,4,128,128]{3,2,1,0:T(8,128)(2,1)S(1)}, u32[]{:S(2)}, u32[]{:S(2)}) collective-permute-start(bf16[1,4,128,128]{3,2,1,0:T(8,128)(2,1)S(1)} %collective-permute-done.6), channel_id=1, source_target_pairs={{0,2},{2,4},{4,6},{6,8},{8,10},{10,12},{12,14},{14,16},{16,18},{18... | collective-permute-start | bytes 393224 | tf_op jit(solution)/shard_map/ppermute | solution.py:70
  221.4 9.4 %collective-permute-start.9 = (bf16[1,4,128,128]{3,2,1,0:T(8,128)(2,1)S(1)}, bf16[1,4,128,128]{3,2,1,0:T(8,128)(2,1)S(1)}, u32[]{:S(2)}, u32[]{:S(2)}) collective-permute-start(bf16[1,4,128,128]{3,2,1,0:T(8,128)(2,1)S(1)} %collective-permute-done.7), channel_id=1, source_target_pairs={{0,30},{2,0},{4,2},{6,4},{8,6},{10,8},{12,10},{14,12},{16,14},{18,... | collective-permute-start | bytes 393224 | tf_op jit(solution)/shard_map/ppermute | solution.py:78
  230.8 9.6 %collective-permute-start.10 = (bf16[1,4,128,128]{3,2,1,0:T(8,128)(2,1)S(1)}, bf16[1,4,128,128]{3,2,1,0:T(8,128)(2,1)S(1)}, u32[]{:S(2)}, u32[]{:S(2)}) collective-permute-start(bf16[1,4,128,128]{3,2,1,0:T(8,128)(2,1)S(1)} %collective-permute-done.8), channel_id=1, source_target_pairs={{0,2},{2,4},{4,6},{6,8},{8,10},{10,12},{12,14},{14,16},{16,18},{18... | collective-permute-start | bytes 393224 | tf_op jit(solution)/shard_map/ppermute | solution.py:70
  230.8 9.6 %collective-permute-start.11 = (bf16[1,4,128,128]{3,2,1,0:T(8,128)(2,1)S(1)}, bf16[1,4,128,128]{3,2,1,0:T(8,128)(2,1)S(1)}, u32[]{:S(2)}, u32[]{:S(2)}) collective-permute-start(bf16[1,4,128,128]{3,2,1,0:T(8,128)(2,1)S(1)} %collective-permute-done.9), channel_id=1, source_target_pairs={{0,30},{2,0},{4,2},{6,4},{8,6},{10,8},{12,10},{14,12},{16,14},{18,... | collective-permute-start | bytes 393224 | tf_op jit(solution)/shard_map/ppermute | solution.py:78
  240.4 8.7 %collective-permute-start.12 = (bf16[1,4,128,128]{3,2,1,0:T(8,128)(2,1)S(1)}, bf16[1,4,128,128]{3,2,1,0:T(8,128)(2,1)S(1)}, u32[]{:S(2)}, u32[]{:S(2)}) collective-permute-start(bf16[1,4,128,128]{3,2,1,0:T(8,128)(2,1)S(1)} %collective-permute-done.10), channel_id=1, source_target_pairs={{0,2},{2,4},{4,6},{6,8},{8,10},{10,12},{12,14},{14,16},{16,18},{18... | collective-permute-start | bytes 393224 | tf_op jit(solution)/shard_map/ppermute | solution.py:70
  240.4 8.7 %collective-permute-start.13 = (bf16[1,4,128,128]{3,2,1,0:T(8,128)(2,1)S(1)}, bf16[1,4,128,128]{3,2,1,0:T(8,128)(2,1)S(1)}, u32[]{:S(2)}, u32[]{:S(2)}) collective-permute-start(bf16[1,4,128,128]{3,2,1,0:T(8,128)(2,1)S(1)} %collective-permute-done.11), channel_id=1, source_target_pairs={{0,30},{2,0},{4,2},{6,4},{8,6},{10,8},{12,10},{14,12},{16,14},{18,... | collective-permute-start | bytes 393224 | tf_op jit(solution)/shard_map/ppermute | solution.py:78
  249.1 8.6 %collective-permute-start.14 = (bf16[1,4,128,128]{3,2,1,0:T(8,128)(2,1)S(1)}, bf16[1,4,128,128]{3,2,1,0:T(8,128)(2,1)S(1)}, u32[]{:S(2)}, u32[]{:S(2)}) collective-permute-start(bf16[1,4,128,128]{3,2,1,0:T(8,128)(2,1)S(1)} %collective-permute-done.12), channel_id=1, source_target_pairs={{0,2},{2,4},{4,6},{6,8},{8,10},{10,12},{12,14},{14,16},{16,18},{18... | collective-permute-start | bytes 393224 | tf_op jit(solution)/shard_map/ppermute | solution.py:70
Sparse Core Ops, SparseCore 0:
  13.5 144.4 all-reduce.1
